TPU v7x, 128 devices: a whole 4x4x4 slice. The times are simulated.
128 devices in a mesh: row: 8 (over y, core), col: 16 (over x, z).
Axes of the slice: x: 4, y: 4, z: 4, core: 2. Of those that a mesh axis runs over, the one named last changes fastest.
Arguments:
- parent_front: float32 [4, 8, 256, 2, 16, 256], P(None, 'row', None, None, 'col'), may hold values from -6 to 48, as said below
- child_tiles: bfloat16 [128, 64, 256, 256], P(('row', 'col')), may hold values from -6 to 6
- tile_target: int32 [128, 64, 2], replicated, may hold values from 0 to 31, as said below
Outputs:
- factored_front: float32 [4, 8, 256, 2, 16, 256], P(None, 'row', None, None, 'col')
Inputs may be any that keep to these rules, and one draw needn't show every extreme that they name: The leading 6 * 256 rows and columns of parent_front form a symmetric matrix with diagonal entries in 32 to 48 and other entries of magnitude at most 30 / 1536. tile_target[d, s] is the parent tile (row, column) into which tile s of device d is added (device d is mesh row d // 16, column d % 16); rows are 6 or more. Parent tile (I, J) lives on mesh row I % 8, column J % 16. The 64 tiles of one device go to 64 different devices, and one device receives a tile from every device.
All inputs are finite; a program needn't handle non-finite values.
Results may differ from a plain program's by a relative error of at most 0.0003.
Values may be sent and summed in bfloat16 or wider, within the bound.
No kernel may reach another device: no remote copies, remote signals or barrier semaphores. Data moves between devices by JAX's collectives and lax.ppermute only.
A program may use at most 192 MiB of HBM per device.

v0:
```python
import jax
import jax.numpy as jnp
from jax import lax
from jax.sharding import PartitionSpec as P

PANELS = 6


def broadcast(shard, axis, root):
    mine = lax.axis_index(axis) == root
    return lax.psum(jnp.where(mine, shard, jnp.zeros_like(shard)), axis)


def shards(parent_front, child_tiles, tile_target):
    lrows = parent_front.shape[0]
    tile = parent_front.shape[2]
    lcols = parent_front.shape[3]
    row_count = lax.axis_size("row")
    col_count = lax.axis_size("col")
    devices = row_count * col_count
    my_row = lax.axis_index("row")
    my_col = lax.axis_index("col")
    myself = my_row * col_count + my_col
    front = parent_front.reshape(lrows, tile, lcols, tile)
    stored = child_tiles.shape[1]
    held = child_tiles.reshape(stored, tile, tile)
    rows_all = tile_target[:, :, 0]
    cols_all = tile_target[:, :, 1]
    owner_all = rows_all % row_count * col_count + cols_all % col_count
    local_all = rows_all // row_count * lcols + cols_all // col_count
    peers = jnp.arange(devices, dtype=jnp.int32)
    my_owner = lax.dynamic_index_in_dim(owner_all, myself, 0, keepdims=False)
    sending = my_owner[None, :] == peers[:, None]
    present = jnp.any(sending, axis=1)
    picked = jnp.sum(jnp.where(sending, jnp.arange(stored, dtype=jnp.int32)[None, :], 0), axis=1)
    outgoing = jnp.where(present[:, None, None], held[picked], jnp.zeros((), jnp.bfloat16))
    arrived = lax.all_to_all(outgoing, ("row", "col"), split_axis=0, concat_axis=0, tiled=True)
    landing = owner_all == myself
    came = jnp.any(landing, axis=1)
    where_to = jnp.sum(jnp.where(landing, local_all, 0), axis=1)
    slots = jnp.arange(lrows * lcols, dtype=jnp.int32)
    onehot = ((where_to[:, None] == slots[None, :]) & came[:, None]).astype(jnp.bfloat16)
    onehot = onehot.reshape(devices, lrows, lcols)
    summed = jnp.einsum("dij,dxy->ixjy", onehot, arrived, preferred_element_type=jnp.float32)
    front = front + summed
    row_ids = my_row + row_count * jnp.arange(lrows, dtype=jnp.int32)
    col_ids = my_col + col_count * jnp.arange(lcols, dtype=jnp.int32)
    stride = col_count // row_count
    pick_rows = my_col // row_count + stride * jnp.arange(lcols, dtype=jnp.int32)
    for step in range(PANELS):
        pivot = broadcast(
            front[step // row_count, :, step // col_count, :], "row", step % row_count
        )
        lower = jnp.linalg.cholesky(pivot)
        column = front[:, :, step // col_count, :].reshape(lrows * tile, tile)
        solved = jax.scipy.linalg.solve_triangular(lower, column.T, lower=True).T.reshape(
            lrows, tile, tile
        )
        factor = jnp.where((row_ids == step)[:, None, None], lower[None, :, :], solved)
        factor = jnp.where((row_ids >= step)[:, None, None], factor, jnp.zeros((), jnp.float32))
        row_panel = broadcast(factor, "col", step % col_count)
        chosen = row_panel[pick_rows]
        col_panel = broadcast(chosen, "row", my_col % row_count)
        update = jnp.einsum("iak,jbk->iajb", row_panel, col_panel, precision=lax.Precision.HIGHEST)
        trailing = front - update
        upper_zero = (row_ids[:, None] == step) & (col_ids[None, :] > step)
        trailing = jnp.where(upper_zero[:, None, :, None], jnp.zeros((), jnp.float32), trailing)
        front = jnp.where(
            (col_ids == step)[None, None, :, None], row_panel[:, :, None, :], trailing
        )
    return front.reshape(parent_front.shape)


def solution(mesh):
    return jax.shard_map(
        shards,
        mesh=mesh,
        in_specs=(
            P(None, "row", None, None, "col", None),
            P(("row", "col"), None, None, None),
            P(),
        ),
        out_specs=P(None, "row", None, None, "col", None),
        check_vma=False,
    )
```

profile of v0, /device:TPU:0, one launch (start us, length us, event | category | flops | bytes accessed | tf_op | source)
XLA Modules:
  0.0 2021.7 jit_solution(16761109816391972855)
XLA Ops:
  49.8 232.3 %all-to-all-done = bf16[128,256,256]{2,1,0:T(8,128)(2,1)} async-done(((bf16[128,256,256]{2,1,0:T(8,128)(2,1)}), bf16[128,256,256]{2,1,0:T(8,128)(2,1)}, u32[]{:S(2)}, u32[]{:S(2)}) %all-to-all-start) | async-done | bytes 16777248 | tf_op jit(solution)/shard_map/all_to_all | solution.py:37
  305.7 55.9 %all-reduce.20.cloned.1.call-done = f32[256,256]{0,1:T(8,128)} async-done(((f32[256,256]{0,1:T(8,128)}), f32[256,256]{0,1:T(8,128)}) %all-reduce.20.cloned.1.call-update) | async-done | bytes 262160 | tf_op jit(solution)/shard_map/psum | solution.py:11
  409.1 20.5 %custom-call.22 = f32[2,128,128]{1,2,0:T(8,128)S(1)} custom-call(f32[2,128,128]{2,1,0:T(8,128)} %copy-done.21), custom_call_target="InvertDiagBlocksLowerTriangular" | custom-call | tf_op jit(solution)/shard_map/jit(_solve_triangular)/triangular_solve | solution.py:56
  435.4 85.3 %all-reduce.22.cloned.1.call-done = f32[4,256,256]{2,1,0:T(8,128)} async-done(((f32[4,256,256]{2,1,0:T(8,128)}), f32[4,256,256]{2,1,0:T(8,128)}) %all-reduce.22.cloned.1.call-update) | async-done | bytes 1048592 | tf_op jit(solution)/shard_map/psum | solution.py:11
  526.8 58.1 %all-reduce.24.cloned.1.call-done = f32[2,256,256]{2,1,0:T(8,128)} async-done(((f32[2,256,256]{2,1,0:T(8,128)}), f32[2,256,256]{2,1,0:T(8,128)}) %all-reduce.24.cloned.1.call-update) | async-done | bytes 524304 | tf_op jit(solution)/shard_map/psum | solution.py:11
  592.2 57.3 %all-reduce.26.cloned.1.call-done = f32[256,256]{0,1:T(8,128)} async-done(((f32[256,256]{0,1:T(8,128)}), f32[256,256]{0,1:T(8,128)}) %all-reduce.26.cloned.1.call-update) | async-done | bytes 262160 | tf_op jit(solution)/shard_map/psum | solution.py:11
  692.6 19.7 custom-call.24
  715.9 86.3 %all-reduce.28.cloned.1.call-done = f32[4,256,256]{2,1,0:T(8,128)} async-done(((f32[4,256,256]{2,1,0:T(8,128)}), f32[4,256,256]{2,1,0:T(8,128)}) %all-reduce.28.cloned.1.call-update) | async-done | bytes 1048592 | tf_op jit(solution)/shard_map/psum | solution.py:11
  806.5 58.6 %all-reduce.30.cloned.1.call-done = f32[2,256,256]{2,1,0:T(8,128)} async-done(((f32[2,256,256]{2,1,0:T(8,128)}), f32[2,256,256]{2,1,0:T(8,128)}) %all-reduce.30.cloned.1.call-update) | async-done | bytes 524304 | tf_op jit(solution)/shard_map/psum | solution.py:11
  873.0 55.9 %all-reduce.32.cloned.1.call-done = f32[256,256]{0,1:T(8,128)} async-done(((f32[256,256]{0,1:T(8,128)}), f32[256,256]{0,1:T(8,128)}) %all-reduce.32.cloned.1.call-update) | async-done | bytes 262160 | tf_op jit(solution)/shard_map/psum | solution.py:11
  976.8 20.5 %custom-call.26 = f32[2,128,128]{1,2,0:T(8,128)S(1)} custom-call(f32[2,128,128]{2,1,0:T(8,128)} %copy-done.22), custom_call_target="InvertDiagBlocksLowerTriangular" | custom-call | tf_op jit(solution)/shard_map/jit(_solve_triangular)/triangular_solve | solution.py:56
  1003.0 86.3 %all-reduce.34.cloned.1.call-done = f32[4,256,256]{2,1,0:T(8,128)} async-done(((f32[4,256,256]{2,1,0:T(8,128)}), f32[4,256,256]{2,1,0:T(8,128)}) %all-reduce.34.cloned.1.call-update) | async-done | bytes 1048592 | tf_op jit(solution)/shard_map/psum | solution.py:11
  1095.4 58.1 %all-reduce.36.cloned.1.call-done = f32[2,256,256]{2,1,0:T(8,128)} async-done(((f32[2,256,256]{2,1,0:T(8,128)}), f32[2,256,256]{2,1,0:T(8,128)}) %all-reduce.36.cloned.1.call-update) | async-done | bytes 524304 | tf_op jit(solution)/shard_map/psum | solution.py:11
  1160.8 57.3 %all-reduce.38.cloned.1.call-done = f32[256,256]{0,1:T(8,128)} async-done(((f32[256,256]{0,1:T(8,128)}), f32[256,256]{0,1:T(8,128)}) %all-reduce.38.cloned.1.call-update) | async-done | bytes 262160 | tf_op jit(solution)/shard_map/psum | solution.py:11
  1261.3 19.7 custom-call.28
  1284.6 86.3 %all-reduce.40.cloned.1.call-done = f32[4,256,256]{2,1,0:T(8,128)} async-done(((f32[4,256,256]{2,1,0:T(8,128)}), f32[4,256,256]{2,1,0:T(8,128)}) %all-reduce.40.cloned.1.call-update) | async-done | bytes 1048592 | tf_op jit(solution)/shard_map/psum | solution.py:11
  1377.1 58.1 %all-reduce.42.cloned.1.call-done = f32[2,256,256]{2,1,0:T(8,128)} async-done(((f32[2,256,256]{2,1,0:T(8,128)}), f32[2,256,256]{2,1,0:T(8,128)}) %all-reduce.42.cloned.1.call-update) | async-done | bytes 524304 | tf_op jit(solution)/shard_map/psum | solution.py:11
  1442.5 57.3 %all-reduce.44.cloned.1.call-done = f32[256,256]{0,1:T(8,128)} async-done(((f32[256,256]{0,1:T(8,128)}), f32[256,256]{0,1:T(8,128)}) %all-reduce.44.cloned.1.call-update) | async-done | bytes 262160 | tf_op jit(solution)/shard_map/psum | solution.py:11
  1566.1 86.3 %all-reduce.46.cloned.1.call-done = f32[4,256,256]{2,1,0:T(8,128)} async-done(((f32[4,256,256]{2,1,0:T(8,128)}), f32[4,256,256]{2,1,0:T(8,128)}) %all-reduce.46.cloned.1.call-update) | async-done | bytes 1048592 | tf_op jit(solution)/shard_map/psum | solution.py:11
  1656.6 58.6 %all-reduce.48.cloned.1.call-done = f32[2,256,256]{2,1,0:T(8,128)} async-done(((f32[2,256,256]{2,1,0:T(8,128)}), f32[2,256,256]{2,1,0:T(8,128)}) %all-reduce.48.cloned.1.call-update) | async-done | bytes 524304 | tf_op jit(solution)/shard_map/psum | solution.py:11
  1723.2 55.9 %all-reduce.50.cloned.1.call-done = f32[256,256]{0,1:T(8,128)} async-done(((f32[256,256]{0,1:T(8,128)}), f32[256,256]{0,1:T(8,128)}) %all-reduce.50.cloned.1.call-update) | async-done | bytes 262160 | tf_op jit(solution)/shard_map/psum | solution.py:11
  1827.2 20.5 %custom-call.32 = f32[2,128,128]{1,2,0:T(8,128)S(1)} custom-call(f32[2,128,128]{2,1,0:T(8,128)} %copy-done.20), custom_call_target="InvertDiagBlocksLowerTriangular" | custom-call | tf_op jit(solution)/shard_map/jit(_solve_triangular)/triangular_solve | solution.py:56
  1853.5 86.3 %all-reduce.52.cloned.1.call-done = f32[4,256,256]{2,1,0:T(8,128)} async-done(((f32[4,256,256]{2,1,0:T(8,128)}), f32[4,256,256]{2,1,0:T(8,128)}) %all-reduce.52.cloned.1.call-update) | async-done | bytes 1048592 | tf_op jit(solution)/shard_map/psum | solution.py:11
  1945.8 58.2 %all-reduce.54.cloned.1.call-done = f32[2,256,256]{2,1,0:T(8,128)} async-done(((f32[2,256,256]{2,1,0:T(8,128)}), f32[2,256,256]{2,1,0:T(8,128)}) %all-reduce.54.cloned.1.call-update) | async-done | bytes 524304 | tf_op jit(solution)/shard_map/psum | solution.py:11
  (349 shorter events, 486.2 us)
Async XLA Ops:
  33.4 12.2 copy-start.10
  33.4 248.6 %all-to-all-start = ((bf16[128,256,256]{2,1,0:T(8,128)(2,1)}), bf16[128,256,256]{2,1,0:T(8,128)(2,1)}, u32[]{:S(2)}, u32[]{:S(2)}) async-start(bf16[128,256,256]{2,1,0:T(8,128)(2,1)} %broadcast_select_fusion), calls=%async_computation | async-start | bytes 33554432 | tf_op jit(solution)/shard_map/all_to_all | solution.py:37
  45.1 316.5 %all-reduce.20.cloned.1.call-start = ((), (), s32[]{:S(2)}) async-start(), calls=%async_computation.1 | async-start | bytes 524288 | tf_op jit(solution)/shard_map/psum | solution.py:11
  302.0 218.7 %all-reduce.22.cloned.1.call-start = ((), (), s32[]{:S(2)}) async-start(), calls=%async_computation.2 | async-start | bytes 2097152 | tf_op jit(solution)/shard_map/psum | solution.py:11
  435.3 149.6 %all-reduce.24.cloned.1.call-start = ((), (), s32[]{:S(2)}) async-start(), calls=%async_computation.3 | async-start | bytes 1048576 | tf_op jit(solution)/shard_map/psum | solution.py:11
  525.3 124.2 %all-reduce.26.cloned.1.call-start = ((), (), s32[]{:S(2)}) async-start(), calls=%async_computation.4 | async-start | bytes 524288 | tf_op jit(solution)/shard_map/psum | solution.py:11
  590.3 211.9 %all-reduce.28.cloned.1.call-start = ((), (), s32[]{:S(2)}) async-start(), calls=%async_computation.5 | async-start | bytes 2097152 | tf_op jit(solution)/shard_map/psum | solution.py:11
  692.6 21.7 %copy-start.23 = (s32[2,2]{1,0:T(2,128)}, s32[2,2]{1,0:T(2,128)S(1)}, u32[]{:S(2)}) copy-start(s32[2,2]{1,0:T(2,128)S(1)} %get-tuple-element.529) | copy-start | bytes 52
  715.9 149.2 %all-reduce.30.cloned.1.call-start = ((), (), s32[]{:S(2)}) async-start(), calls=%async_computation.6 | async-start | bytes 1048576 | tf_op jit(solution)/shard_map/psum | solution.py:11
  805.0 123.9 %all-reduce.32.cloned.1.call-start = ((), (), s32[]{:S(2)}) async-start(), calls=%async_computation.7 | async-start | bytes 524288 | tf_op jit(solution)/shard_map/psum | solution.py:11
  869.8 219.5 %all-reduce.34.cloned.1.call-start = ((), (), s32[]{:S(2)}) async-start(), calls=%async_computation.8 | async-start | bytes 2097152 | tf_op jit(solution)/shard_map/psum | solution.py:11
  1003.0 150.6 %all-reduce.36.cloned.1.call-start = ((), (), s32[]{:S(2)}) async-start(), calls=%async_computation.9 | async-start | bytes 1048576 | tf_op jit(solution)/shard_map/psum | solution.py:11
  1093.9 124.2 %all-reduce.38.cloned.1.call-start = ((), (), s32[]{:S(2)}) async-start(), calls=%async_computation.10 | async-start | bytes 524288 | tf_op jit(solution)/shard_map/psum | solution.py:11
  1158.9 211.9 %all-reduce.40.cloned.1.call-start = ((), (), s32[]{:S(2)}) async-start(), calls=%async_computation.11 | async-start | bytes 2097152 | tf_op jit(solution)/shard_map/psum | solution.py:11
  1160.8 95.9 %copy-start.24 = (s32[2,2]{1,0:T(2,128)S(1)}, s32[2,2]{1,0:T(2,128)}, u32[]{:S(2)}) copy-start(s32[2,2]{1,0:T(2,128)} %get-tuple-element.530) | copy-start | bytes 52
  1284.5 150.7 %all-reduce.42.cloned.1.call-start = ((), (), s32[]{:S(2)}) async-start(), calls=%async_computation.12 | async-start | bytes 1048576 | tf_op jit(solution)/shard_map/psum | solution.py:11
  1373.6 61.6 %copy-start.2 = (f32[4,256,2,256]{1,3,2,0:T(8,128)S(1)}, f32[4,256,2,256]{1,3,2,0:T(8,128)}, u32[]{:S(2)}) copy-start(f32[4,256,2,256]{1,3,2,0:T(8,128)} %copy-done.1) | copy-start | bytes 6291460
  1375.6 124.2 %all-reduce.44.cloned.1.call-start = ((), (), s32[]{:S(2)}) async-start(), calls=%async_computation.13 | async-start | bytes 524288 | tf_op jit(solution)/shard_map/psum | solution.py:11
  1440.7 211.7 %all-reduce.46.cloned.1.call-start = ((), (), s32[]{:S(2)}) async-start(), calls=%async_computation.14 | async-start | bytes 2097152 | tf_op jit(solution)/shard_map/psum | solution.py:11
  1542.7 21.7 %copy-start.25 = (s32[2,2]{1,0:T(2,128)}, s32[2,2]{1,0:T(2,128)S(1)}, u32[]{:S(2)}) copy-start(s32[2,2]{1,0:T(2,128)S(1)} %get-tuple-element.532) | copy-start | bytes 52
  1566.0 149.2 %all-reduce.48.cloned.1.call-start = ((), (), s32[]{:S(2)}) async-start(), calls=%async_computation.15 | async-start | bytes 1048576 | tf_op jit(solution)/shard_map/psum | solution.py:11
  1655.2 124.0 %all-reduce.50.cloned.1.call-start = ((), (), s32[]{:S(2)}) async-start(), calls=%async_computation.16 | async-start | bytes 524288 | tf_op jit(solution)/shard_map/psum | solution.py:11
  1719.9 219.8 %all-reduce.52.cloned.1.call-start = ((), (), s32[]{:S(2)}) async-start(), calls=%async_computation.17 | async-start | bytes 2097152 | tf_op jit(solution)/shard_map/psum | solution.py:11
  1853.4 150.6 %all-reduce.54.cloned.1.call-start = ((), (), s32[]{:S(2)}) async-start(), calls=%async_computation.18 | async-start | bytes 1048576 | tf_op jit(solution)/shard_map/psum | solution.py:11
  (24 other events, 51.7 us)
Sparse Core Ops, SparseCore 0:
  302.2 59.4 all-reduce.19
  435.4 85.2 all-reduce.21
  525.4 59.4 all-reduce.23
  590.4 59.0 all-reduce.25
  716.0 86.2 all-reduce.27
  805.2 59.8 all-reduce.29
  869.9 58.9 all-reduce.31
  1003.1 86.2 all-reduce.33
  1094.0 59.4 all-reduce.35
  1159.1 59.0 all-reduce.37
  1284.6 86.2 all-reduce.39
  1375.8 59.4 all-reduce.41
  1440.8 59.0 all-reduce.43
  1566.1 86.2 all-reduce.45
  1655.3 59.8 all-reduce.47
  1720.1 59.0 all-reduce.49
  1853.5 86.2 all-reduce.51
  1944.5 59.4 all-reduce.53
where the time goes:
time: 2030 us; the launch traced here: 2020 us
  waiting for transfers between devices  1440 us (71%)
  other arithmetic  379 us (19%)
  local copies, waits for them, and re-layouts  108 us (5%)
  matrix products  56.6 us (3%)
  between operations  22.6 us (1%)
    psum x18, waiting for transfers between devices, broadcast(): return lax.psum(jnp.where(mine, shard, jnp.zeros_like(shard)), axis)  1210 us
    all_to_all x1, waiting for transfers between devices, shards(): lax.all_to_all(outgoing, ('row', 'col'), split_axis=0, concat_axis=0, til...  232 us
    another operation x41, other arithmetic, shards(): lower = jnp.linalg.cholesky(pivot)  207 us
    another operation x13, other arithmetic, shards(): jax.scipy.linalg.solve_triangular(lower, column.T, lower=True)  124 us
  transfers between devices with their start and end apart: 19, of which 19 were waited for; matrix products, arithmetic and copies ran while one was open for 1% of the time, Pallas kernels for 0%

commit v1 on v0

--- a/solution.py
+++ b/solution.py
@@ -8,7 +8,11 @@
 
 def broadcast(shard, axis, root):
     mine = lax.axis_index(axis) == root
-    return lax.psum(jnp.where(mine, shard, jnp.zeros_like(shard)), axis)
+
+    def cover_leaf(local_values):
+        return jnp.sum(lax.all_gather(local_values, axis), 0)
+
+    return cover_leaf(jnp.where(mine, shard, jnp.zeros_like(shard)))
 
 
 def shards(parent_front, child_tiles, tile_target):

time: 2030 us -> 1860 us (0.916)
  waiting for transfers between devices: 1440 us -> 1230 us
  other arithmetic: 379 us -> 445 us
  local copies, waits for them, and re-layouts: 108 us -> 82.8 us
    psum x18 -> x0, waiting for transfers between devices: 1210 us -> none  [broadcast(): return lax.psum(jnp.where(mine, shard, jnp.zeros_like(shard)), axis)]
    all_gather x0 -> x18, waiting for transfers between devices: none -> 990 us  [cover_leaf(): return jnp.sum(lax.all_gather(local_values, axis), 0)]
    reduce_sum x0 -> x18, other arithmetic: none -> 69.4 us  [cover_leaf(): return jnp.sum(lax.all_gather(local_values, axis), 0)]
where the time goes in v1:
time: 1860 us; the launch traced here: 1850 us
  waiting for transfers between devices  1230 us (66%)
  other arithmetic  445 us (24%)
  local copies, waits for them, and re-layouts  82.8 us (4%)
  matrix products  56.7 us (3%)
  between operations  23 us (1%)
    all_gather x18, waiting for transfers between devices, cover_leaf(): return jnp.sum(lax.all_gather(local_values, axis), 0)  990 us
    all_to_all x1, waiting for transfers between devices, shards(): lax.all_to_all(outgoing, ('row', 'col'), split_axis=0, concat_axis=0, til...  236 us
    another operation x41, other arithmetic, shards(): lower = jnp.linalg.cholesky(pivot)  207 us
    another operation x13, other arithmetic, shards(): jax.scipy.linalg.solve_triangular(lower, column.T, lower=True)  121 us
    reduce_sum x18, other arithmetic, cover_leaf(): return jnp.sum(lax.all_gather(local_values, axis), 0)  69.4 us
  transfers between devices with their start and end apart: 19, of which 19 were waited for; matrix products, arithmetic and copies ran while one was open for 1% of the time, Pallas kernels for 0%

profile of v1, /device:TPU:0, one launch (start us, length us, event | category | flops | bytes accessed | tf_op | source)
XLA Modules:
  0.0 1850.2 jit_solution(13681476094822794583)
XLA Ops:
  45.7 236.4 %all-to-all-done = bf16[128,256,256]{2,1,0:T(8,128)(2,1)} async-done(((bf16[128,256,256]{2,1,0:T(8,128)(2,1)}), bf16[128,256,256]{2,1,0:T(8,128)(2,1)}, u32[]{:S(2)}, u32[]{:S(2)}) %all-to-all-start) | async-done | bytes 16777248 | tf_op jit(solution)/shard_map/all_to_all | solution.py:41
  300.8 23.9 %all-gather.43.cloned.1.call-done = f32[8,256,1,256]{3,1,2,0:T(8,128)} async-done(((f32[1,256,1,256]{3,1,2,0:T(8,128)}), f32[8,256,1,256]{3,1,2,0:T(8,128)}) %all-gather.43.cloned.1.call-update) | async-done | bytes 2097168 | tf_op jit(solution)/shard_map/all_gather | solution.py:13
  366.9 19.7 %custom-call.22 = f32[2,128,128]{1,2,0:T(8,128)S(1)} custom-call(f32[2,128,128]{2,1,0:T(8,128)S(1)} %get-tuple-element.45), custom_call_target="InvertDiagBlocksLowerTriangular" | custom-call | tf_op jit(solution)/shard_map/jit(_solve_triangular)/triangular_solve | solution.py:60
  390.2 111.8 %all-gather.31.cloned.1.call-done = f32[16,4,256,256]{3,2,1,0:T(8,128)} async-done(((f32[1,4,256,256]{3,2,1,0:T(8,128)}), f32[16,4,256,256]{3,2,1,0:T(8,128)}) %all-gather.31.cloned.1.call-update) | async-done | bytes 16777232 | tf_op jit(solution)/shard_map/all_gather | solution.py:13
  511.7 30.6 %all-gather.45.cloned.1.call-done = f32[16,256,256]{2,1,0:T(8,128)} async-done(((f32[2,256,256]{2,1,0:T(8,128)}), f32[16,256,256]{2,1,0:T(8,128)}) %all-gather.45.cloned.1.call-update) | async-done | bytes 4194320 | tf_op jit(solution)/shard_map/all_gather | solution.py:13
  552.8 24.0 %all-gather.47.cloned.1.call-done = f32[8,256,1,256]{3,1,2,0:T(8,128)} async-done(((f32[1,256,1,256]{3,1,2,0:T(8,128)}), f32[8,256,1,256]{3,1,2,0:T(8,128)}) %all-gather.47.cloned.1.call-update) | async-done | bytes 2097168 | tf_op jit(solution)/shard_map/all_gather | solution.py:13
  619.4 19.7 %custom-call.24 = f32[2,128,128]{1,2,0:T(8,128)S(1)} custom-call(f32[2,128,128]{2,1,0:T(8,128)S(1)} %get-tuple-element.46), custom_call_target="InvertDiagBlocksLowerTriangular" | custom-call | tf_op jit(solution)/shard_map/jit(_solve_triangular)/triangular_solve | solution.py:60
  642.7 111.9 %all-gather.33.cloned.1.call-done = f32[16,4,256,256]{3,2,1,0:T(8,128)} async-done(((f32[1,4,256,256]{3,2,1,0:T(8,128)}), f32[16,4,256,256]{3,2,1,0:T(8,128)}) %all-gather.33.cloned.1.call-update) | async-done | bytes 16777232 | tf_op jit(solution)/shard_map/all_gather | solution.py:13
  764.2 30.6 %all-gather.49.cloned.1.call-done = f32[16,256,256]{2,1,0:T(8,128)} async-done(((f32[2,256,256]{2,1,0:T(8,128)}), f32[16,256,256]{2,1,0:T(8,128)}) %all-gather.49.cloned.1.call-update) | async-done | bytes 4194320 | tf_op jit(solution)/shard_map/all_gather | solution.py:13
  807.2 21.9 %all-gather.51.cloned.1.call-done = f32[8,256,1,256]{3,1,2,0:T(8,128)} async-done(((f32[1,256,1,256]{3,1,2,0:T(8,128)}), f32[8,256,1,256]{3,1,2,0:T(8,128)}) %all-gather.51.cloned.1.call-update) | async-done | bytes 2097168 | tf_op jit(solution)/shard_map/all_gather | solution.py:13
  878.4 20.5 %custom-call.26 = f32[2,128,128]{1,2,0:T(8,128)S(1)} custom-call(f32[2,128,128]{2,1,0:T(8,128)} %copy-done.18), custom_call_target="InvertDiagBlocksLowerTriangular" | custom-call | tf_op jit(solution)/shard_map/jit(_solve_triangular)/triangular_solve | solution.py:60
  904.6 111.9 %all-gather.35.cloned.1.call-done = f32[16,4,256,256]{3,2,1,0:T(8,128)} async-done(((f32[1,4,256,256]{3,2,1,0:T(8,128)}), f32[16,4,256,256]{3,2,1,0:T(8,128)}) %all-gather.35.cloned.1.call-update) | async-done | bytes 16777232 | tf_op jit(solution)/shard_map/all_gather | solution.py:13
  1029.9 28.2 %all-gather.53.cloned.1.call-done = f32[16,256,256]{2,1,0:T(8,128)} async-done(((f32[2,256,256]{2,1,0:T(8,128)}), f32[16,256,256]{2,1,0:T(8,128)}) %all-gather.53.cloned.1.call-update) | async-done | bytes 4194320 | tf_op jit(solution)/shard_map/all_gather | solution.py:13
  1071.4 24.2 %all-gather.55.cloned.1.call-done = f32[8,256,1,256]{3,1,2,0:T(8,128)} async-done(((f32[1,256,1,256]{3,1,2,0:T(8,128)}), f32[8,256,1,256]{3,1,2,0:T(8,128)}) %all-gather.55.cloned.1.call-update) | async-done | bytes 2097168 | tf_op jit(solution)/shard_map/all_gather | solution.py:13
  1138.3 19.7 %custom-call.28 = f32[2,128,128]{1,2,0:T(8,128)S(1)} custom-call(f32[2,128,128]{2,1,0:T(8,128)S(1)} %get-tuple-element.48), custom_call_target="InvertDiagBlocksLowerTriangular" | custom-call | tf_op jit(solution)/shard_map/jit(_solve_triangular)/triangular_solve | solution.py:60
  1161.6 111.9 %all-gather.37.cloned.1.call-done = f32[16,4,256,256]{3,2,1,0:T(8,128)} async-done(((f32[1,4,256,256]{3,2,1,0:T(8,128)}), f32[16,4,256,256]{3,2,1,0:T(8,128)}) %all-gather.37.cloned.1.call-update) | async-done | bytes 16777232 | tf_op jit(solution)/shard_map/all_gather | solution.py:13
  1283.1 30.6 %all-gather.57.cloned.1.call-done = f32[16,256,256]{2,1,0:T(8,128)} async-done(((f32[2,256,256]{2,1,0:T(8,128)}), f32[16,256,256]{2,1,0:T(8,128)}) %all-gather.57.cloned.1.call-update) | async-done | bytes 4194320 | tf_op jit(solution)/shard_map/all_gather | solution.py:13
  1324.2 24.0 %all-gather.59.cloned.1.call-done = f32[8,256,1,256]{3,1,2,0:T(8,128)} async-done(((f32[1,256,1,256]{3,1,2,0:T(8,128)}), f32[8,256,1,256]{3,1,2,0:T(8,128)}) %all-gather.59.cloned.1.call-update) | async-done | bytes 2097168 | tf_op jit(solution)/shard_map/all_gather | solution.py:13
  1414.2 111.9 %all-gather.39.cloned.1.call-done = f32[16,4,256,256]{3,2,1,0:T(8,128)} async-done(((f32[1,4,256,256]{3,2,1,0:T(8,128)}), f32[16,4,256,256]{3,2,1,0:T(8,128)}) %all-gather.39.cloned.1.call-update) | async-done | bytes 16777232 | tf_op jit(solution)/shard_map/all_gather | solution.py:13
  1535.7 30.6 %all-gather.61.cloned.1.call-done = f32[16,256,256]{2,1,0:T(8,128)} async-done(((f32[2,256,256]{2,1,0:T(8,128)}), f32[16,256,256]{2,1,0:T(8,128)}) %all-gather.61.cloned.1.call-update) | async-done | bytes 4194320 | tf_op jit(solution)/shard_map/all_gather | solution.py:13
  1578.7 21.9 %all-gather.63.cloned.1.call-done = f32[8,256,1,256]{3,1,2,0:T(8,128)} async-done(((f32[1,256,1,256]{3,1,2,0:T(8,128)}), f32[8,256,1,256]{3,1,2,0:T(8,128)}) %all-gather.63.cloned.1.call-update) | async-done | bytes 2097168 | tf_op jit(solution)/shard_map/all_gather | solution.py:13
  1650.1 20.5 %custom-call.32 = f32[2,128,128]{1,2,0:T(8,128)S(1)} custom-call(f32[2,128,128]{2,1,0:T(8,128)} %copy-done.19), custom_call_target="InvertDiagBlocksLowerTriangular" | custom-call | tf_op jit(solution)/shard_map/jit(_solve_triangular)/triangular_solve | solution.py:60
  1676.3 111.9 %all-gather.41.cloned.1.call-done = f32[16,4,256,256]{3,2,1,0:T(8,128)} async-done(((f32[1,4,256,256]{3,2,1,0:T(8,128)}), f32[16,4,256,256]{3,2,1,0:T(8,128)}) %all-gather.41.cloned.1.call-update) | async-done | bytes 16777232 | tf_op jit(solution)/shard_map/all_gather | solution.py:13
  1801.5 28.2 %all-gather.65.cloned.1.call-done = f32[16,256,256]{2,1,0:T(8,128)} async-done(((f32[2,256,256]{2,1,0:T(8,128)}), f32[16,256,256]{2,1,0:T(8,128)}) %all-gather.65.cloned.1.call-update) | async-done | bytes 4194320 | tf_op jit(solution)/shard_map/all_gather | solution.py:13
  (379 shorter events, 527.8 us)
Async XLA Ops:
  33.4 248.6 %all-to-all-start = ((bf16[128,256,256]{2,1,0:T(8,128)(2,1)}), bf16[128,256,256]{2,1,0:T(8,128)(2,1)}, u32[]{:S(2)}, u32[]{:S(2)}) async-start(bf16[128,256,256]{2,1,0:T(8,128)(2,1)} %broadcast_select_fusion), calls=%async_computation | async-start | bytes 33554432 | tf_op jit(solution)/shard_map/all_to_all | solution.py:41
  45.1 279.6 %all-gather.43.cloned.1.call-start = ((), (), s32[]{:S(2)}) async-start(), calls=%async_computation.7 | async-start | bytes 2359296 | tf_op jit(solution)/shard_map/all_gather | solution.py:13
  299.8 202.2 %all-gather.31.cloned.1.call-start = ((), (), s32[]{:S(2)}) async-start(), calls=%async_computation.1 | async-start | bytes 17825792 | tf_op jit(solution)/shard_map/all_gather | solution.py:13
  390.1 152.2 %all-gather.45.cloned.1.call-start = ((), (), s32[]{:S(2)}) async-start(), calls=%async_computation.8 | async-start | bytes 4718592 | tf_op jit(solution)/shard_map/all_gather | solution.py:13
  510.4 66.3 %all-gather.47.cloned.1.call-start = ((), (), s32[]{:S(2)}) async-start(), calls=%async_computation.9 | async-start | bytes 2359296 | tf_op jit(solution)/shard_map/all_gather | solution.py:13
  551.5 203.1 %all-gather.33.cloned.1.call-start = ((), (), s32[]{:S(2)}) async-start(), calls=%async_computation.2 | async-start | bytes 17825792 | tf_op jit(solution)/shard_map/all_gather | solution.py:13
  619.4 21.7 %copy-start.20 = (s32[2,2]{1,0:T(2,128)}, s32[2,2]{1,0:T(2,128)S(1)}, u32[]{:S(2)}) copy-start(s32[2,2]{1,0:T(2,128)S(1)} %get-tuple-element.519) | copy-start | bytes 52
  642.6 152.2 %all-gather.49.cloned.1.call-start = ((), (), s32[]{:S(2)}) async-start(), calls=%async_computation.10 | async-start | bytes 4718592 | tf_op jit(solution)/shard_map/all_gather | solution.py:13
  763.0 66.1 %all-gather.51.cloned.1.call-start = ((), (), s32[]{:S(2)}) async-start(), calls=%async_computation.11 | async-start | bytes 2359296 | tf_op jit(solution)/shard_map/all_gather | solution.py:13
  803.8 212.6 %all-gather.35.cloned.1.call-start = ((), (), s32[]{:S(2)}) async-start(), calls=%async_computation.3 | async-start | bytes 17825792 | tf_op jit(solution)/shard_map/all_gather | solution.py:13
  904.6 153.5 %all-gather.53.cloned.1.call-start = ((), (), s32[]{:S(2)}) async-start(), calls=%async_computation.12 | async-start | bytes 4718592 | tf_op jit(solution)/shard_map/all_gather | solution.py:13
  1026.7 68.9 %all-gather.55.cloned.1.call-start = ((), (), s32[]{:S(2)}) async-start(), calls=%async_computation.13 | async-start | bytes 2359296 | tf_op jit(solution)/shard_map/all_gather | solution.py:13
  1061.5 4.6 copy-start.11
  1070.3 203.1 %all-gather.37.cloned.1.call-start = ((), (), s32[]{:S(2)}) async-start(), calls=%async_computation.4 | async-start | bytes 17825792 | tf_op jit(solution)/shard_map/all_gather | solution.py:13
  1097.4 36.7 %copy-start.21 = (s32[2,2]{1,0:T(2,128)S(1)}, s32[2,2]{1,0:T(2,128)}, u32[]{:S(2)}) copy-start(s32[2,2]{1,0:T(2,128)} %get-tuple-element.520) | copy-start | bytes 52
  1161.5 152.2 %all-gather.57.cloned.1.call-start = ((), (), s32[]{:S(2)}) async-start(), calls=%async_computation.14 | async-start | bytes 4718592 | tf_op jit(solution)/shard_map/all_gather | solution.py:13
  1281.9 66.3 %all-gather.59.cloned.1.call-start = ((), (), s32[]{:S(2)}) async-start(), calls=%async_computation.15 | async-start | bytes 2359296 | tf_op jit(solution)/shard_map/all_gather | solution.py:13
  1322.9 203.1 %all-gather.39.cloned.1.call-start = ((), (), s32[]{:S(2)}) async-start(), calls=%async_computation.5 | async-start | bytes 17825792 | tf_op jit(solution)/shard_map/all_gather | solution.py:13
  1390.9 21.7 %copy-start.22 = (s32[2,2]{1,0:T(2,128)}, s32[2,2]{1,0:T(2,128)S(1)}, u32[]{:S(2)}) copy-start(s32[2,2]{1,0:T(2,128)S(1)} %get-tuple-element.522) | copy-start | bytes 52
  1414.1 152.2 %all-gather.61.cloned.1.call-start = ((), (), s32[]{:S(2)}) async-start(), calls=%async_computation.16 | async-start | bytes 4718592 | tf_op jit(solution)/shard_map/all_gather | solution.py:13
  1534.5 66.1 %all-gather.63.cloned.1.call-start = ((), (), s32[]{:S(2)}) async-start(), calls=%async_computation.17 | async-start | bytes 2359296 | tf_op jit(solution)/shard_map/all_gather | solution.py:13
  1575.3 212.9 %all-gather.41.cloned.1.call-start = ((), (), s32[]{:S(2)}) async-start(), calls=%async_computation.6 | async-start | bytes 17825792 | tf_op jit(solution)/shard_map/all_gather | solution.py:13
  1676.3 153.5 %all-gather.65.cloned.1.call-start = ((), (), s32[]{:S(2)}) async-start(), calls=%async_computation.18 | async-start | bytes 4718592 | tf_op jit(solution)/shard_map/all_gather | solution.py:13
  1833.2 4.6 copy-start.10
  (19 other events, 42.8 us)
Sparse Core Ops, SparseCore 0:
  299.9 24.7 all-gather.42
  390.2 111.7 all-gather.30
  510.5 31.6 all-gather.44
  551.6 25.0 all-gather.46
  642.8 111.7 all-gather.32
  763.1 31.6 all-gather.48
  803.9 25.1 all-gather.50
  904.7 111.7 all-gather.34
  1026.9 31.1 all-gather.52
  1070.5 25.1 all-gather.54
  1161.6 111.7 all-gather.36
  1282.0 31.6 all-gather.56
  1323.0 25.0 all-gather.58
  1414.2 111.7 all-gather.38
  1534.6 31.6 all-gather.60
  1575.4 25.0 all-gather.62
  1676.4 111.7 all-gather.40
  1798.6 31.1 all-gather.64
